TPU v7x, 32 devices: a whole 2x2x4 slice. The times are simulated.
32 devices in a mesh: sect: 4 (over y, x), tile: 8 (over z, core).
Axes of the slice: x: 2, y: 2, z: 4, core: 2. Of those that a mesh axis runs over, the one named last changes fastest.
Arguments:
- zonal: float32 [4, 64, 512], P('sect', 'tile'), may hold values from -1.5 to 1.5
- merid: float32 [4, 64, 512], P('sect', 'tile'), may hold values from -1.5 to 1.5
- height: float32 [4, 64, 512], P('sect', 'tile'), may hold values from -6 to 6
- level_kappa: float32 [4], replicated, may hold values from 0.2 to 2
- sea: int32 [64, 512], P('tile'), may hold values 0 or 1
- flags: int32 [4, 64, 512], P(None, 'tile', 'sect'), may hold values 0 or 1
- conc: float32 [12, 4, 64, 512], P(None, None, 'tile', 'sect'), may hold values from 0.1 to 2
- react: float32 [12, 12], replicated, may hold values from -1.2 to 1.2
- absorb: float32 [12], replicated, may hold values from 0.05 to 1
- light: float32 [4], replicated, may hold values from 0.1 to 1
Outputs:
- conc_out: float32 [12, 4, 64, 512], P(None, None, 'tile', 'sect')
- zonal_out: float32 [4, 64, 512], P('sect', 'tile')
- merid_out: float32 [4, 64, 512], P('sect', 'tile')
- height_out: float32 [4, 64, 512], P('sect', 'tile')
All inputs are finite; a program needn't handle non-finite values. No bound on the sum of `sea` or of `flags` on one device may be relied on, other than what follows from the above.
Results may differ from a plain program's by a relative error of at most 0.00022.
Values sent between devices are 32-bit elements; how exact they have to be, the bound alone decides.
A program may use at most 64 MiB of HBM per device.

v0:
```python
import functools

import jax
import jax.numpy as jnp
from jax import lax
from jax.experimental import pallas as pl
from jax.experimental.pallas import tpu as pltpu
from jax.sharding import PartitionSpec as P

STEPS = 4
INTERVALS = 2

time_step = 0.1
gravity = 1.0
coriolis = 0.3
viscosity = 0.05
heat_coupling = 0.05
tracer_step = 0.5
stir_gain = 4.0

LANES = 128
EDGE = 4 * STEPS
NEAR = EDGE // 2
FIRST = 4
SECOND = 2


def ocean_steps(zonal, merid, height, wet, forced, keep):
    tall, wide = zonal.shape

    def east(a):
        return pltpu.roll(a, wide - 1, 1)

    def west(a):
        return pltpu.roll(a, 1, 1)

    def north(a):
        return pltpu.roll(a, tall - 1, 0)

    def south(a):
        return pltpu.roll(a, 1, 0)

    keep_rate = time_step * viscosity
    self_rate = 1.0 / keep_rate - 4.0
    turn_rate = time_step * coriolis / keep_rate
    steep = 0.5 * gravity * time_step / keep_rate
    gain = keep_rate * wet
    rise = steep * height
    if forced is not None:
        forced = steep * forced
    zonal_sum = merid_sum = None
    for step in range(STEPS):
        ze, zw, zn, zs = east(zonal), west(zonal), north(zonal), south(zonal)
        me, mw, mn, ms = east(merid), west(merid), north(merid), south(merid)
        rise = rise - (0.5 * time_step * steep) * ((ze - zw) + (mn - ms))
        zonal_part = ((ze + zw) + (zn + zs)) + (self_rate * zonal + turn_rate * merid)
        merid_part = ((me + mw) + (mn + ms)) + (self_rate * merid - turn_rate * zonal)
        if forced is not None:
            rise = rise + forced
        zonal_new = gain * (zonal_part - (east(rise) - west(rise)))
        merid_new = gain * (merid_part - (north(rise) - south(rise)))
        zonal, merid = zonal_new, merid_new
        zonal_sum = zonal[keep] if step == 0 else zonal_sum + zonal[keep]
        merid_sum = merid[keep] if step == 0 else merid_sum + merid[keep]
    return zonal[keep], merid[keep], (1.0 / steep) * rise[keep], zonal_sum / STEPS, merid_sum / STEPS


def column_terms(speeds, upwind, half_wet, kappa_in):
    levels = len(speeds)
    kappa, stencil = [], []
    for k in range(levels):
        along_x, along_y = speeds[k]
        kappa.append(kappa_in[k] * (1.0 + stir_gain * (along_x * along_x + along_y * along_y)))
        terms = []
        for speed in (along_x, along_y):
            terms.append(half_wet * jnp.where(upwind[k], jnp.maximum(speed, 0.0), 0.5 * speed))
            terms.append(half_wet * jnp.where(upwind[k], jnp.minimum(speed, 0.0), 0.5 * speed))
        stencil.append(terms)
    couple = [tracer_step * 0.5 * (kappa[k] + kappa[k + 1]) for k in range(levels - 1)]
    out, factor = [], None
    for k in range(levels):
        denom = 1.0
        if k > 0:
            denom = denom + couple[k - 1]
        if k < levels - 1:
            denom = denom + couple[k]
        if k > 0:
            denom = denom + couple[k - 1] * factor
        inverse = 1.0 / denom
        px, qx, py, qy = stencil[k]
        out.append(
            dict(
                centre=inverse * (1.0 - ((px - qx) + (py - qy))),
                west=inverse * px,
                east=inverse * qx,
                south=inverse * py,
                north=inverse * qy,
                lower=inverse * couple[k - 1] if k > 0 else None,
                upper=inverse * couple[k] if k < levels - 1 else None,
            )
        )
        factor = -out[k]["upper"] if k < levels - 1 else None
    return out


def solve_column(terms, cells):
    levels = len(terms)
    partial = []
    for k in range(levels):
        t = terms[k]
        base, west, east, south, north = cells(k)
        now = t["centre"] * base + (t["west"] * west - t["east"] * east) + (t["south"] * south - t["north"] * north)
        if k > 0:
            now = now + t["lower"] * partial[k - 1]
        partial.append(now)
    for k in range(levels - 2, -1, -1):
        partial[k] = partial[k] + terms[k]["upper"] * partial[k + 1]
    return partial


def kernel(
    sects,
    tiles,
    zonal_in,
    merid_in,
    height_in,
    sea_in,
    flags_in,
    conc_in,
    kappa_hbm,
    react_hbm,
    absorb_hbm,
    light_hbm,
    conc_out,
    zonal_out,
    merid_out,
    height_out,
    kappa_in,
    react_in,
    absorb_in,
    light_in,
    own,
    sea,
    flags,
    conc,
    react_d,
    base,
    west_v,
    east_v,
    south_v,
    north_v,
    cols_send,
    cols_recv,
    rows_send,
    rows_recv,
    blk_send,
    blk_recv,
    sea_send,
    sea_recv,
    mix_send,
    mix_recv,
    rest_send,
    rest_recv,
    strip_send,
    strip_recv,
    wet_all,
    state,
    state_edge,
    means,
    last_means,
    force,
    out_send,
    out_recv,
    local_sem,
    blk_ssem,
    blk_rsem,
    sea_ssem,
    sea_rsem,
    mix_ssem,
    mix_rsem,
    state_ssem,
    state_rsem,
    force_ssem,
    force_rsem,
    strip_ssem,
    strip_rsem,
    halo_ssem,
    halo_rsem,
    out_ssem,
    out_rsem,
    known_sem,
):
    me_s = lax.axis_index("sect")
    me_t = lax.axis_index("tile")
    tracers, levels, rows, columns = conc_in.shape
    depth = zonal_in.shape[0]
    bands = 3
    far = bands

    def sect_at(offset):
        return lax.rem(me_s + (offset + sects), sects)

    def tile_at(offset):
        return lax.rem(me_t + (offset + tiles), tiles)

    def hops(s, t):
        count = t // 2
        for bit in range((sects - 1).bit_length()):
            count = count + lax.rem(s // (1 << bit), 2)
        return count

    def place(s, t):
        return ((2 * hops(s, t) + 1 - lax.rem(t, 2)) * tiles + t) * sects + s

    def across(m):
        s = me_s
        for bit in range((sects - 1).bit_length()):
            if m >> bit & 1:
                s = s + (1 << bit) - 2 * (1 << bit) * lax.rem(me_s // (1 << bit), 2)
        return s

    near = sorted(range(sects), key=lambda m: (m.bit_count(), m))
    peers = [(m, across(m), dt, tile_at(dt)) for dt in (1, 0, -1) for m in near if m or dt]
    mine = place(me_s, me_t)
    later, sooner, greet = [], [], []
    for m, s, dt, t in peers:
        is_later = place(s, t) > mine
        if m and dt:
            wraps = (me_t + dt < 0) | (me_t + dt >= tiles)
            ahead = hops(s, t) - hops(me_s, me_t)
            mutual = wraps & (ahead <= 1) & (ahead >= -1)
            later.append(is_later & jnp.logical_not(mutual))
            sooner.append(jnp.logical_not(is_later) & jnp.logical_not(mutual))
            greet.append(is_later | mutual)
        else:
            later.append(is_later)
            sooner.append(jnp.logical_not(is_later))
            greet.append(is_later)

    def remote(src, dst, send, recv, to_s, to_t):
        return pltpu.make_async_remote_copy(
            src_ref=src,
            dst_ref=dst,
            send_sem=send,
            recv_sem=recv,
            device_id=(to_s, to_t),
            device_id_type=pl.DeviceIdType.MESH,
        )

    fields_in = (zonal_in, merid_in, height_in)
    ocean_local = [pltpu.make_async_copy(field, own.at[f], local_sem.at[f]) for f, field in enumerate(fields_in)]
    ocean_local.append(pltpu.make_async_copy(sea_in, sea, local_sem.at[3]))
    tracer_local = [
        pltpu.make_async_copy(src, dst, local_sem.at[4 + i])
        for i, (src, dst) in enumerate(
            (
                (conc_in, conc),
                (flags_in, flags),
                (react_hbm, react_in),
                (absorb_hbm, absorb_in),
                (kappa_hbm, kappa_in),
                (light_hbm, light_in),
            )
        )
    ]
    barrier = pltpu.get_barrier_semaphore()
    @pl.when(me_t == 0)
    def _():
        for s in [across(m) for m in near[::-1]]:
            pl.semaphore_signal(barrier, inc=1, device_id=(s, tiles - 2), device_id_type=pl.DeviceIdType.MESH)

    heard = 0
    for n, (_, s, _, t) in reversed(list(enumerate(peers))):
        heard = heard + jnp.where(later[n], 0, 1)

        @pl.when(greet[n])
        def _():
            pl.semaphore_signal(barrier, inc=1, device_id=(s, t), device_id_type=pl.DeviceIdType.MESH)

    for copy in ocean_local + tracer_local:
        copy.start()
    heard = heard + jnp.where(me_t == tiles - 2, sects, 0)

    @pl.when(heard > 0)
    def _():
        pl.semaphore_wait(barrier, heard)

    for n, (_, s, dt, t) in enumerate(peers):

        @pl.when(sooner[n])
        def _():
            pl.semaphore_signal(
                known_sem.at[1 - dt, me_s], inc=1, device_id=(s, t), device_id_type=pl.DeviceIdType.MESH
            )

    lane = lax.broadcasted_iota(jnp.int32, (rows, columns), 1)
    row = lax.broadcasted_iota(jnp.int32, (rows, columns), 0)
    low_half = lane < LANES // 2

    for copy in ocean_local:
        copy.wait()

    def lanes_of(s):
        return slice((s % sects) * columns, (s % sects + 1) * columns)

    sea_f = [sea[:, lanes_of(s)].astype(jnp.float32) for s in range(sects)]
    for d in range(sects):
        for ld in range(depth):
            packed = None
            for f in range(4):
                if f < 3:
                    blk_send[d, 4 * ld + f] = own[f, ld, :, lanes_of(d)]
                    after, before = own[f, ld, :, lanes_of(d + 1)], own[f, ld, :, lanes_of(d - 1)]
                else:
                    after, before = sea_f[(d + 1) % sects], sea_f[(d - 1) % sects]
                edge = jnp.where(low_half, after, before)
                if f == 0:
                    packed = edge
                else:
                    inside = (lane >= 2 * EDGE * f - EDGE) & (lane < 2 * EDGE * f + EDGE)
                    packed = jnp.where(inside, pltpu.roll(edge, 2 * EDGE * f, 1), packed)
            blk_send[d, 4 * ld + 3] = packed
    own_columns = pl.ds(pl.multiple_of(me_s * columns, LANES), columns)
    wet_cols = sea[:, own_columns].astype(jnp.float32)
    is_wet = wet_cols == 1.0
    sea_send[...] = wet_cols

    def blk_copy(j, s_slot, send, to_s, to_t, src):
        return remote(blk_send.at[src], blk_recv.at[j, s_slot], send, blk_rsem.at[j, s_slot], to_s, to_t)

    sent = []
    to_peer = [
        blk_copy(1 - dt, me_s, blk_ssem.at[1 + dt, s], s, t, s) for _, s, dt, t in peers
    ]
    seas = [
        remote(sea_send, sea_recv.at[1 - dt], sea_ssem.at[1 + dt], sea_rsem.at[1 - dt], me_s, tile_at(dt))
        for dt in (1, -1)
    ]
    over = [blk_copy(far, me_s, blk_ssem.at[far, across(m)], across(m), 0, across(m)) for m in near[::-1]]
    over.append(remote(sea_send, sea_recv.at[far], sea_ssem.at[far], sea_rsem.at[far], me_s, 0))

    @pl.when(me_t == tiles - 2)
    def _():
        for copy in over[sects:] + over[:sects]:
            copy.start()

    def begin(n):
        m, _, dt, _ = peers[n]
        if not m:
            seas[0 if dt == 1 else 1].start()
        to_peer[n].start()

    for n in sorted(range(len(peers)), key=lambda n: (-peers[n][2] % bands, -n)):

        @pl.when(jnp.logical_not(later[n]))
        def _():
            begin(n)

    blk_recv[1, me_s] = blk_send[me_s]
    sea_recv[1] = sea_send[...]
    for copy in tracer_local:
        copy.wait()

    cells = tracers * levels

    def react_and_pack(turn, heated):
        names = tracers + (1 if heated else 0)
        to_east = [jnp.zeros((rows, columns), jnp.float32) for _ in range(pl.cdiv(cells, LANES))]
        to_west = list(to_east)
        for k in range(levels):
            old = [conc[i, k] for i in range(tracers)]
            heat_d = None
            for i in range(names):
                n = i * levels + k
                if i < tracers:
                    growth = react_in[i, 0] * old[0]
                    for j in range(1, tracers):
                        growth = growth + react_in[i, j] * old[j]
                    new = old[i] + tracer_step * growth
                    kept = jnp.where(is_wet, new, old[i])
                    if heated:
                        a = absorb_in[i]
                        heat_d = a * new if i == 0 else heat_d + a * new
                        heat_b = a * kept if i == 0 else heat_b + a * kept
                else:
                    mix_send[k] = heat_d
                    rest_send[k] = heat_b
                    continue
                react_d[n] = new
                base[n] = kept
                rows_send[turn, 0, pl.ds(n, 1)] = new[rows - 1 : rows]
                rows_send[turn, 1, pl.ds(n, 1)] = new[0:1]
                p, at = divmod(n, LANES)
                here = lane == at
                turned = pltpu.roll(new, (at + 1) % columns, 1)
                to_east[p] = jnp.where(here, turned, to_east[p])
                turned = pltpu.roll(new, at, 1) if at else new
                to_west[p] = jnp.where(here, turned, to_west[p])
        for p in range(len(to_east)):
            cols_send[turn, 0, p] = to_east[p]
            cols_send[turn, 1, p] = to_west[p]
        copies = []
        for i, d in enumerate((1, -1)):
            copies.append(
                remote(
                    rows_send.at[turn, i],
                    rows_recv.at[turn, i],
                    halo_ssem.at[turn, i],
                    halo_rsem.at[turn, i],
                    me_s,
                    tile_at(d),
                )
            )
            copies.append(
                remote(
                    cols_send.at[turn, i],
                    cols_recv.at[turn, i],
                    halo_ssem.at[turn, 2 + i],
                    halo_rsem.at[turn, 2 + i],
                    sect_at(d),
                    me_t,
                )
            )
        return copies

    def shift_cells(turn):
        from_west = [cols_recv[turn, 0, p] for p in range(pl.cdiv(cells, LANES))]
        from_east = [cols_recv[turn, 1, p] for p in range(pl.cdiv(cells, LANES))]
        for n in range(cells):
            p, at = divmod(n, LANES)
            new = react_d[n]
            edge = pltpu.roll(from_west[p], columns - at, 1) if at else from_west[p]
            west_v[n] = jnp.where(lane == 0, edge, pltpu.roll(new, 1, 1))
            edge = pltpu.roll(from_east[p], columns - 1 - at, 1) if at < columns - 1 else from_east[p]
            east_v[n] = jnp.where(lane == columns - 1, edge, pltpu.roll(new, columns - 1, 1))
            edge = jnp.broadcast_to(rows_recv[turn, 0, pl.ds(n, 1)], (rows, columns))
            south_v[n] = jnp.where(row == 0, edge, pltpu.roll(new, 1, 0))
            edge = jnp.broadcast_to(rows_recv[turn, 1, pl.ds(n, 1)], (rows, columns))
            north_v[n] = jnp.where(row == rows - 1, edge, pltpu.roll(new, rows - 1, 0))

    def tracer_cells(i):
        def read(k):
            n = i * levels + k
            return base[n], west_v[n], east_v[n], south_v[n], north_v[n]

        return read

    halo0 = react_and_pack(0, True)
    for k in range(levels):
        rest_send[levels + k] = flags[k].astype(jnp.float32)
    per = LANES // NEAR
    for p in range(pl.cdiv(3 * levels, per)):
        to_east = to_west = jnp.zeros((rows, columns), jnp.float32)
        for at in range(min(per, 3 * levels - p * per)):
            q = p * per + at
            value = mix_send[q] if q < levels else rest_send[q - levels]
            here = (lane >= NEAR * at) & (lane < NEAR * at + NEAR)
            turned = pltpu.roll(value, (NEAR * at + NEAR) % LANES, 1)
            to_east = jnp.where(here, turned, to_east)
            turned = pltpu.roll(value, NEAR * at, 1) if at else value
            to_west = jnp.where(here, turned, to_west)
        strip_send[0, p] = to_east
        strip_send[1, p] = to_west
    sent.extend(seas)
    mixes, strips = [], []
    for i, dt in enumerate((1, -1)):
        mixes.append(remote(mix_send, mix_recv.at[i], mix_ssem.at[i], mix_rsem.at[i], me_s, tile_at(dt)))
    for i, ds in enumerate((1, -1)):
        for dt in (1, -1, 0):
            strips.append(
                remote(
                    strip_send.at[i],
                    strip_recv.at[i, 1 - dt],
                    strip_ssem.at[i, 1 - dt],
                    strip_rsem.at[i, 1 - dt],
                    sect_at(ds),
                    tile_at(dt),
                )
            )
    sent.extend(mixes + strips + halo0)
    for now in (1, 0, -1):
        for n, (_, s, dt, _) in enumerate(peers):
            if dt == now:

                @pl.when(later[n])
                def _():
                    pl.semaphore_wait(known_sem.at[1 + dt, s], 1)
                    begin(n)

        if now == 1:
            continue
        directions = (1, 0) if now == 0 else (-1,)
        for dt in directions:
            if dt:
                mixes[0 if dt == 1 else 1].start()
                halo0[0 if dt == 1 else 2].start()
            else:
                halo0[1].start()
                halo0[3].start()
            for i in range(2):
                strips[3 * i + (1, -1, 0).index(dt)].start()

    rest = remote(rest_send, rest_recv, mix_ssem.at[2], mix_rsem.at[2], me_s, 0)

    @pl.when(me_t == tiles - 1)
    def _():
        rest.start()


    for copy in seas:
        copy.wait_recv()

    def blk_wait(j, s):
        blk_copy(j, s, blk_ssem.at[0, 0], me_s, me_t, me_s).wait_recv()

    for j in (0, 2):
        blk_wait(j, me_s)
    in_edge = (lane < EDGE) | (lane >= LANES - EDGE)

    def wet_band(j):
        turned = pltpu.roll(blk_recv[j, me_s, 3], LANES - 6 * EDGE, 1)
        return jnp.concatenate([sea_recv[j], jnp.where(in_edge, turned, 0.0)], axis=1)

    for j in range(bands):
        wet_all[j * rows : (j + 1) * rows] = wet_band(j)
    centre = slice(rows, 2 * rows)

    def first_levels(group, slots, wet, target):
        for l in [group * FIRST * depth + ld for ld in range(FIRST * depth)]:
            s, ld = l // depth, lax.rem(l, depth)
            full = []
            packed = [blk_recv[j, s, 4 * ld + 3] for j in slots]
            for f in range(3):
                parts = []
                for j, pack in zip(slots, packed):
                    turned = pltpu.roll(pack, LANES - 2 * EDGE * f, 1) if f else pack
                    parts.append(jnp.concatenate([blk_recv[j, s, 4 * ld + f], turned], axis=1))
                full.append(jnp.concatenate(parts, axis=0))
            z, m, h, zm, mm = ocean_steps(*full, wet, None, (centre, slice(None)))
            for f, value in enumerate((z, m, h)):
                state[target, 3 * l + f] = value[:, 0:columns]
                state_edge[target, 3 * l + f] = value[:, columns:]
            for i, value in enumerate((zm, mm)):
                means[target, l, i] = value

    def first_interval(group, carry):
        for s in [group * FIRST + at for at in range(FIRST)]:

            @pl.when(s != me_s)
            def _():
                for j in range(bands):
                    blk_wait(j, s)

        first_levels(group, (0, 1, 2), wet_all[...], 1)
        return carry

    def beyond_interval(group, carry):
        for at in range(FIRST):
            blk_wait(far, group * FIRST + at)
        first_levels(group, (far, 0, 1), jnp.concatenate([wet_band(far), wet_all[0 : 2 * rows]], axis=0), 0)
        return carry

    lax.fori_loop(0, sects // FIRST, first_interval, 0)

    pair = LANES // (2 * NEAR)

    def pack_edges(buffer, slot, values):
        start = buffer.shape[1] - pl.cdiv(len(values), pair)
        for p in range(pl.cdiv(len(values), pair)):
            tile = values[p * pair]
            for i, value in enumerate(values[p * pair + 1 : (p + 1) * pair], 1):
                here = (lane >= 2 * NEAR * i - NEAR) & (lane < 2 * NEAR * i + NEAR)
                tile = jnp.where(here, pltpu.roll(value, 2 * NEAR * i, 1), tile)
            buffer[slot, start + p] = tile

    def with_edges(buffer, slot, q, count):
        start = buffer.shape[1] - pl.cdiv(count, pair)
        p, at = divmod(q, pair)
        edge = buffer[slot, start + p]
        if at:
            edge = pltpu.roll(edge, LANES - 2 * NEAR * at, 1)
        return jnp.concatenate([buffer[slot, q], edge], axis=1)

    pack_edges(state, 1, [state_edge[1, q] for q in range(3 * levels)])

    def neighbours(buffer, send, recv):
        return [
            remote(buffer.at[1], buffer.at[0], send.at[0], recv.at[0], me_s, tile_at(1)),
            remote(buffer.at[1], buffer.at[2], send.at[1], recv.at[1], me_s, tile_at(-1)),
        ]

    states = neighbours(state, state_ssem, state_rsem)
    forces = neighbours(force, force_ssem, force_rsem)

    def hand_on(copies):
        copies[1].start()

        @pl.when(me_t != tiles - 1)
        def _():
            copies[0].start()

    hand_on(states)
    for copy in mixes + strips:
        copy.wait_recv()

    def wide_tile(q, j):
        p, at = divmod(q, per)
        if j == 1:
            inner = mix_send[q] if q < levels else rest_send[q - levels]
        elif q < levels:
            inner = mix_recv[j // 2, q]
        else:
            inner = rest_recv[q - levels]
        west_part = pltpu.roll(strip_recv[0, j, p], LANES - NEAR - NEAR * at, 1)
        east_part = strip_recv[1, j, p]
        if at:
            east_part = pltpu.roll(east_part, LANES - NEAR * at, 1)
        return jnp.concatenate([inner, jnp.where(low_half, east_part, west_part)], axis=1)

    wide = columns + LANES

    def heat_band(j):
        speeds = [(means[j, k, 0], means[j, k, 1]) for k in range(levels)]
        upwind = [wide_tile(2 * levels + k, j) > 0.5 for k in range(levels)]
        terms = column_terms(speeds, upwind, tracer_step * wet_all[j * rows : (j + 1) * rows], kappa_in)
        band = slice(j * rows, (j + 1) * rows)

        def heat_cells(k):
            each = [wide_tile(k, i) for i in range(bands)]
            d = jnp.concatenate(each, axis=0)
            return (
                wide_tile(levels + k, j),
                pltpu.roll(each[j], 1, 1),
                pltpu.roll(each[j], wide - 1, 1),
                pltpu.roll(d, 1, 0)[band],
                pltpu.roll(d, bands * rows - 1, 0)[band],
            )

        edges = []
        for k, value in enumerate(solve_column(terms, heat_cells)):
            value = (time_step * heat_coupling) * (light_in[k] * value)
            force[j, k] = value[:, 0:columns]
            edges.append(value[:, columns:])
        pack_edges(force, j, edges)

    heat_band(1)
    hand_on(forces)

    half_wet = tracer_step * wet_cols
    upwind = [flags[k] == 1 for k in range(levels)]
    speeds = [tuple(means[1, k, i, :, 0:columns] for i in range(2)) for k in range(levels)]
    terms = column_terms(speeds, upwind, half_wet, kappa_in)
    for copy in halo0:
        copy.wait_recv()
    shift_cells(0)
    for i in range(tracers):
        for k, value in enumerate(solve_column(terms, tracer_cells(i))):
            conc[i, k] = value
    halo1 = react_and_pack(1, False)
    for copy in halo1:
        copy.start()
    sent.extend(halo1)

    @pl.when(me_t == 0)
    def _():
        over[sects].wait_recv()
        lax.fori_loop(0, sects // FIRST, beyond_interval, 0)
        pack_edges(state, 0, [state_edge[0, q] for q in range(3 * levels)])
        rest.wait_recv()
        heat_band(0)

    states[1].wait_recv()
    forces[1].wait_recv()

    @pl.when(me_t != 0)
    def _():
        states[0].wait_recv()
        forces[0].wait_recv()

    def out_copy(l):
        owner, ld = l // depth, l % depth
        return remote(
            out_send.at[l], out_recv.at[me_s, ld], out_ssem.at[l], out_rsem.at[me_s, ld], owner, me_t
        )

    def second_interval(group):
        for l in [group * SECOND + at for at in range(SECOND)]:
            whole = [
                jnp.concatenate([with_edges(state, j, 3 * l + f, 3 * levels) for j in range(bands)], axis=0)
                for f in range(3)
            ]
            forced = jnp.concatenate([with_edges(force, j, l, levels) for j in range(bands)], axis=0)
            z, m, h, zm, mm = ocean_steps(*whole, wet_all[...], forced, (centre, slice(0, columns)))
            last_means[l, 0] = zm
            last_means[l, 1] = mm
            for f, value in enumerate((z, m, h)):
                out_send[l, f] = value
        for l in [group * SECOND + at for at in range(SECOND)]:

            @pl.when(l // depth != me_s)
            def _():
                out_copy(l).start()

    for group in range(levels // SECOND):
        second_interval(group)
    for ld in range(depth):
        out_recv[me_s, ld] = out_send[me_s * depth + ld]

    upwind = [flags[k] == 1 for k in range(levels)]
    speeds = [(last_means[k, 0], last_means[k, 1]) for k in range(levels)]
    terms = column_terms(speeds, upwind, half_wet, kappa_in)
    for copy in halo1:
        copy.wait_recv()
    shift_cells(1)
    for i in range(tracers):
        for k, value in enumerate(solve_column(terms, tracer_cells(i))):
            conc_out[i, k] = value

    def gather(s, carry):
        @pl.when(s != me_s)
        def _():
            for ld in range(depth):
                remote(
                    out_send.at[0], out_recv.at[s, ld], out_ssem.at[0], out_rsem.at[s, ld], me_s, me_t
                ).wait_recv()

        return carry

    lax.fori_loop(0, sects, gather, 0)
    for s in range(sects):
        for ld in range(depth):
            for f, ref in enumerate((zonal_out, merid_out, height_out)):
                ref[ld, :, lanes_of(s)] = out_recv[s, ld, f]
    for copy in sent + [states[1], forces[1]]:
        copy.wait_send()

    for copy in to_peer:
        copy.wait_send()

    @pl.when(me_t != tiles - 1)
    def _():
        states[0].wait_send()
        forces[0].wait_send()

    @pl.when(me_t == tiles - 1)
    def _():
        rest.wait_send()

    @pl.when(me_t == tiles - 2)
    def _():
        for copy in over:
            copy.wait_send()


    def drain(l, carry):
        @pl.when(l // depth != me_s)
        def _():
            out_copy(l).wait_send()

        return carry

    lax.fori_loop(0, levels, drain, 0)


def put_out(*refs):
    copies = [
        pltpu.make_async_copy(src, dst, refs[8].at[i])
        for i, (src, dst) in enumerate(zip(refs[:4], refs[4:8]))
    ]
    for copy in copies:
        copy.start()
    for copy in copies:
        copy.wait()


def body(sects, tiles, zonal, merid, height, level_kappa, sea, flags, conc, react, absorb, light):
    tracers, levels, rows, columns = conc.shape
    depth, _, wide = zonal.shape
    assert rows >= NEAR and columns == LANES and INTERVALS == 2
    assert tiles > 3 and sects > 1 and levels == sects * depth and wide == sects * columns
    cells = tracers * levels
    packs = pl.cdiv(cells, LANES)
    padded = pl.cdiv(cells, 8) * 8
    strips = pl.cdiv(3 * levels, LANES // NEAR)
    pair = LANES // (2 * NEAR)
    f32 = jnp.float32
    dma = pltpu.SemaphoreType.DMA
    any_space = pl.BlockSpec(memory_space=pl.ANY)
    vmem = pl.BlockSpec(memory_space=pltpu.VMEM)
    results = pl.pallas_call(
        functools.partial(kernel, sects, tiles),
        out_shape=[
            pltpu.VMEM(conc.shape, f32),
            pltpu.VMEM(zonal.shape, f32),
            pltpu.VMEM(merid.shape, f32),
            pltpu.VMEM(height.shape, f32),
        ],
        in_specs=[pl.BlockSpec(memory_space=pltpu.HBM)] * 10,
        out_specs=[vmem] * 4,
        scratch_shapes=[
            pltpu.SMEM(level_kappa.shape, f32),
            pltpu.SMEM(react.shape, f32),
            pltpu.SMEM(absorb.shape, f32),
            pltpu.SMEM(light.shape, f32),
            pltpu.VMEM((3, depth, rows, wide), f32),
            pltpu.VMEM((rows, wide), jnp.int32),
            pltpu.VMEM(flags.shape, jnp.int32),
            pltpu.VMEM(conc.shape, f32),
        ]
        + [pltpu.VMEM((cells, rows, columns), f32)] * 6
        + [
            pltpu.VMEM((2, 2, packs, rows, columns), f32),
            pltpu.VMEM((2, 2, packs, rows, columns), f32),
            pltpu.VMEM((2, 2, padded, columns), f32),
            pltpu.VMEM((2, 2, padded, columns), f32),
            pltpu.VMEM((sects, 4 * depth, rows, columns), f32),
            pltpu.VMEM((4, sects, 4 * depth, rows, columns), f32),
            pltpu.VMEM((rows, columns), f32),
            pltpu.VMEM((4, rows, columns), f32),
            pltpu.VMEM((levels, rows, columns), f32),
            pltpu.VMEM((2, levels, rows, columns), f32),
            pltpu.VMEM((2 * levels, rows, columns), f32),
            pltpu.VMEM((2 * levels, rows, columns), f32),
            pltpu.VMEM((2, strips, rows, columns), f32),
            pltpu.VMEM((2, 3, strips, rows, columns), f32),
            pltpu.VMEM((3 * rows, columns + LANES), f32),
            pltpu.VMEM((3, 3 * levels + pl.cdiv(3 * levels, pair), rows, columns), f32),
            pltpu.VMEM((2, 3 * levels, rows, columns), f32),
            pltpu.VMEM((2, levels, 2, rows, columns + LANES), f32),
            pltpu.VMEM((levels, 2, rows, columns), f32),
            pltpu.VMEM((3, levels + pl.cdiv(levels, pair), rows, columns), f32),
            pltpu.VMEM((levels, 3, rows, columns), f32),
            pltpu.VMEM((sects, depth, 3, rows, columns), f32),
            dma((10,)),
            dma((4, sects)),
            dma((4, sects)),
            dma((4,)),
            dma((4,)),
            dma((3,)),
            dma((3,)),
            dma((2,)),
            dma((2,)),
            dma((2,)),
            dma((2,)),
            dma((2, 3)),
            dma((2, 3)),
            dma((2, 4)),
            dma((2, 4)),
            dma((levels,)),
            dma((sects, depth)),
            pltpu.SemaphoreType.REGULAR((3, sects)),
        ],
        compiler_params=pltpu.CompilerParams(collective_id=0, has_side_effects=True),
        name="coupled",
    )(zonal, merid, height, sea, flags, conc, level_kappa, react, absorb, light)
    return pl.pallas_call(
        put_out,
        out_shape=[jax.ShapeDtypeStruct(r.shape, f32) for r in results],
        in_specs=[vmem] * 4,
        out_specs=[any_space] * 4,
        scratch_shapes=[dma((4,))],
        name="put_out",
    )(*[pltpu.with_memory_space_constraint(r, pltpu.VMEM) for r in results])


def solution(mesh):
    placed = (
        P("sect", "tile", None),
        P("sect", "tile", None),
        P("sect", "tile", None),
        P(),
        P("tile", None),
        P(None, "tile", "sect"),
        P(None, None, "tile", "sect"),
        P(),
        P(),
        P(),
    )
    return jax.shard_map(
        functools.partial(body, mesh.shape["sect"], mesh.shape["tile"]),
        mesh=mesh,
        in_specs=placed,
        out_specs=(
            P(None, None, "tile", "sect"),
            P("sect", "tile", None),
            P("sect", "tile", None),
            P("sect", "tile", None),
        ),
        check_vma=False,
    )
```

profile of v0, /device:TPU:0, one launch (start us, length us, event | category | flops | bytes accessed | tf_op | source)
XLA Modules:
  0.0 19.9 jit_solution(171719529750133251)
XLA Ops:
  0.6 18.5 %coupled.1 = (f32[12,4,8,128]{3,2,1,0:T(8,128)S(1)}, f32[1,8,512]{2,1,0:T(8,128)S(1)}, f32[1,8,512]{2,1,0:T(8,128)S(1)}, f32[1,8,512]{2,1,0:T(8,128)S(1)}) custom-call(f32[1,8,512]{2,1,0:T(8,128)} %zonal_in.1, f32[1,8,512]{2,1,0:T(8,128)} %merid_in.1, f32[1,8,512]{2,1,0:T(8,128)} %height_in.1, s32[8,512]{1,0:T(8,128)} %sea_in.1, s32[4,8,128]{2,1,0:T(8,128)} %flags_in.1, ...), custom_call_target="tpu_custom_call" | custom-call | tf_op jit(solution)/shard_map/coupled/pallas_call | solution.py:790
  19.1 0.7 %put_out.1 = (f32[12,4,8,128]{3,2,1,0:T(8,128)}, f32[1,8,512]{2,1,0:T(8,128)}, f32[1,8,512]{2,1,0:T(8,128)}, f32[1,8,512]{2,1,0:T(8,128)}) custom-call(f32[12,4,8,128]{3,2,1,0:T(8,128)S(1)} %get-tuple-element.8.refs_0_, f32[1,8,512]{2,1,0:T(8,128)S(1)} %get-tuple-element.9.refs_1_, f32[1,8,512]{2,1,0:T(8,128)S(1)} %get-tuple-element.10.refs_2_, ...), custom_call_target="tpu_custom_call" | custom-call | tf_op jit(solution)/shard_map/put_out/pallas_call | solution.py:856
where the time goes:
time: 20.1 us; the launch traced here: 19.9 us
  Pallas kernels  19.2 us (96%)
  between operations  0.64 us (3%)
    pallas_call x1, Pallas kernels, body(): pl.pallas_call(functools.partial(kernel, sects, tiles), out_shape=[pltpu....  18.5 us
    pallas_call x1, Pallas kernels, body(): pl.pallas_call(put_out, out_shape=[jax.ShapeDtypeStruct(r.shape, f32) for...  0.72 us

commit v1 on v0

--- a/solution.py
+++ b/solution.py
@@ -159,8 +159,6 @@
     sea_recv,
     mix_send,
     mix_recv,
-    rest_send,
-    rest_recv,
     strip_send,
     strip_recv,
     wet_all,
@@ -203,14 +201,11 @@
     def tile_at(offset):
         return lax.rem(me_t + (offset + tiles), tiles)
 
-    def hops(s, t):
-        count = t // 2
+    def place(s, t):
+        hops = t // 2
         for bit in range((sects - 1).bit_length()):
-            count = count + lax.rem(s // (1 << bit), 2)
-        return count
-
-    def place(s, t):
-        return ((2 * hops(s, t) + 1 - lax.rem(t, 2)) * tiles + t) * sects + s
+            hops = hops + lax.rem(s // (1 << bit), 2)
+        return ((2 * hops + 1 - lax.rem(t, 2)) * tiles + t) * sects + s
 
     def across(m):
         s = me_s
@@ -222,20 +217,17 @@
     near = sorted(range(sects), key=lambda m: (m.bit_count(), m))
     peers = [(m, across(m), dt, tile_at(dt)) for dt in (1, 0, -1) for m in near if m or dt]
     mine = place(me_s, me_t)
-    later, sooner, greet = [], [], []
+    later, sooner, direct, answer = [], [], [], []
     for m, s, dt, t in peers:
-        is_later = place(s, t) > mine
+        spot = place(s, t)
+        later.append(spot > mine)
+        sooner.append(spot < mine)
         if m and dt:
-            wraps = (me_t + dt < 0) | (me_t + dt >= tiles)
-            ahead = hops(s, t) - hops(me_s, me_t)
-            mutual = wraps & (ahead <= 1) & (ahead >= -1)
-            later.append(is_later & jnp.logical_not(mutual))
-            sooner.append(jnp.logical_not(is_later) & jnp.logical_not(mutual))
-            greet.append(is_later | mutual)
+            direct.append(spot > place(me_s, t))
+            answer.append((spot < mine) & (mine > place(s, me_t)))
         else:
-            later.append(is_later)
-            sooner.append(jnp.logical_not(is_later))
-            greet.append(is_later)
+            direct.append(True)
+            answer.append(spot < mine)
 
     def remote(src, dst, send, recv, to_s, to_t):
         return pltpu.make_async_remote_copy(
@@ -273,7 +265,7 @@
     for n, (_, s, _, t) in reversed(list(enumerate(peers))):
         heard = heard + jnp.where(later[n], 0, 1)
 
-        @pl.when(greet[n])
+        @pl.when(later[n])
         def _():
             pl.semaphore_signal(barrier, inc=1, device_id=(s, t), device_id_type=pl.DeviceIdType.MESH)
 
@@ -287,7 +279,7 @@
 
     for n, (_, s, dt, t) in enumerate(peers):
 
-        @pl.when(sooner[n])
+        @pl.when(answer[n])
         def _():
             pl.semaphore_signal(
                 known_sem.at[1 - dt, me_s], inc=1, device_id=(s, t), device_id_type=pl.DeviceIdType.MESH
@@ -339,11 +331,6 @@
     over = [blk_copy(far, me_s, blk_ssem.at[far, across(m)], across(m), 0, across(m)) for m in near[::-1]]
     over.append(remote(sea_send, sea_recv.at[far], sea_ssem.at[far], sea_rsem.at[far], me_s, 0))
 
-    @pl.when(me_t == tiles - 2)
-    def _():
-        for copy in over[sects:] + over[:sects]:
-            copy.start()
-
     def begin(n):
         m, _, dt, _ = peers[n]
         if not m:
@@ -352,9 +339,14 @@
 
     for n in sorted(range(len(peers)), key=lambda n: (-peers[n][2] % bands, -n)):
 
-        @pl.when(jnp.logical_not(later[n]))
+        @pl.when(sooner[n])
         def _():
             begin(n)
+
+    @pl.when(me_t == tiles - 2)
+    def _():
+        for copy in over[sects:] + over[:sects]:
+            copy.start()
 
     blk_recv[1, me_s] = blk_send[me_s]
     sea_recv[1] = sea_send[...]
@@ -384,7 +376,9 @@
                         heat_b = a * kept if i == 0 else heat_b + a * kept
                 else:
                     mix_send[k] = heat_d
-                    rest_send[k] = heat_b
+                    mix_send[levels + k] = heat_b
+                    rows_send[turn, 0, pl.ds(n, 1)] = heat_d[rows - 1 : rows]
+                    rows_send[turn, 1, pl.ds(n, 1)] = heat_d[0:1]
                     continue
                 react_d[n] = new
                 base[n] = kept
@@ -399,12 +393,16 @@
         for p in range(len(to_east)):
             cols_send[turn, 0, p] = to_east[p]
             cols_send[turn, 1, p] = to_west[p]
+        return halo_copies(turn, names * levels)
+
+    def halo_copies(turn, count):
+        tall = pl.cdiv(count, 8) * 8
         copies = []
         for i, d in enumerate((1, -1)):
             copies.append(
                 remote(
-                    rows_send.at[turn, i],
-                    rows_recv.at[turn, i],
+                    rows_send.at[turn, i, pl.ds(0, tall)],
+                    rows_recv.at[turn, i, pl.ds(0, tall)],
                     halo_ssem.at[turn, i],
                     halo_rsem.at[turn, i],
                     me_s,
@@ -447,13 +445,12 @@
 
     halo0 = react_and_pack(0, True)
     for k in range(levels):
-        rest_send[levels + k] = flags[k].astype(jnp.float32)
+        mix_send[2 * levels + k] = flags[k].astype(jnp.float32)
     per = LANES // NEAR
     for p in range(pl.cdiv(3 * levels, per)):
         to_east = to_west = jnp.zeros((rows, columns), jnp.float32)
         for at in range(min(per, 3 * levels - p * per)):
-            q = p * per + at
-            value = mix_send[q] if q < levels else rest_send[q - levels]
+            value = mix_send[p * per + at]
             here = (lane >= NEAR * at) & (lane < NEAR * at + NEAR)
             turned = pltpu.roll(value, (NEAR * at + NEAR) % LANES, 1)
             to_east = jnp.where(here, turned, to_east)
@@ -462,9 +459,7 @@
         strip_send[0, p] = to_east
         strip_send[1, p] = to_west
     sent.extend(seas)
-    mixes, strips = [], []
-    for i, dt in enumerate((1, -1)):
-        mixes.append(remote(mix_send, mix_recv.at[i], mix_ssem.at[i], mix_rsem.at[i], me_s, tile_at(dt)))
+    strips = []
     for i, ds in enumerate((1, -1)):
         for dt in (1, -1, 0):
             strips.append(
@@ -477,30 +472,56 @@
                     tile_at(dt),
                 )
             )
-    sent.extend(mixes + strips + halo0)
-    for now in (1, 0, -1):
-        for n, (_, s, dt, _) in enumerate(peers):
-            if dt == now:
-
-                @pl.when(later[n])
-                def _():
-                    pl.semaphore_wait(known_sem.at[1 + dt, s], 1)
-                    begin(n)
-
-        if now == 1:
-            continue
-        directions = (1, 0) if now == 0 else (-1,)
-        for dt in directions:
-            if dt:
-                mixes[0 if dt == 1 else 1].start()
-                halo0[0 if dt == 1 else 2].start()
-            else:
-                halo0[1].start()
-                halo0[3].start()
-            for i in range(2):
-                strips[3 * i + (1, -1, 0).index(dt)].start()
-
-    rest = remote(rest_send, rest_recv, mix_ssem.at[2], mix_rsem.at[2], me_s, 0)
+    sent.extend(strips + halo0)
+
+    def reach(n, when):
+        _, s, dt, _ = peers[n]
+
+        @pl.when(later[n] & when)
+        def _():
+            @pl.when(direct[n])
+            def _():
+                pl.semaphore_wait(known_sem.at[1 + dt, s], 1)
+
+            begin(n)
+
+    def edges(dt):
+        if dt:
+            halo0[0 if dt == 1 else 2].start()
+        else:
+            halo0[1].start()
+            halo0[3].start()
+        for i in range(2):
+            strips[3 * i + (1, -1, 0).index(dt)].start()
+
+    ready = {}
+    for dt in (1, -1, 0):
+        ready[dt] = True
+        for ds in (0, 1, -1):
+            if ds or dt:
+                ready[dt] = (place(sect_at(ds), tile_at(dt)) < mine) & ready[dt]
+
+        @pl.when(ready[dt])
+        def _():
+            edges(dt)
+
+    for n in sorted(range(len(peers)), key=lambda n: (near.index(peers[n][0]), n)):
+        reach(n, me_t != 0 if peers[n][2] == -1 else True)
+    for dt in (0, 1):
+
+        @pl.when(jnp.logical_not(ready[dt]))
+        def _():
+            edges(dt)
+
+    for n, peer in enumerate(peers):
+        if peer[2] == -1:
+            reach(n, me_t == 0)
+
+    @pl.when(jnp.logical_not(ready[-1]))
+    def _():
+        edges(-1)
+
+    rest = remote(mix_send, mix_recv, mix_ssem.at[0], mix_rsem.at[0], me_s, 0)
 
     @pl.when(me_t == tiles - 1)
     def _():
@@ -600,22 +621,41 @@
             copies[0].start()
 
     hand_on(states)
-    for copy in mixes + strips:
+    half_wet = tracer_step * wet_cols
+
+    def first_tracers():
+        upwind = [flags[k] == 1 for k in range(levels)]
+        speeds = [tuple(means[1, k, i, :, 0:columns] for i in range(2)) for k in range(levels)]
+        terms = column_terms(speeds, upwind, half_wet, kappa_in)
+        shift_cells(0)
+        for i in range(tracers):
+            for k, value in enumerate(solve_column(terms, tracer_cells(i))):
+                conc[i, k] = value
+        for copy in react_and_pack(1, False):
+            copy.start()
+
+    halo1 = halo_copies(1, cells)
+    sent.extend(halo1)
+    for copy in halo0:
         copy.wait_recv()
 
-    def wide_tile(q, j):
+    @pl.when(me_t == 0)
+    def _():
+        first_tracers()
+
+    for copy in strips:
+        copy.wait_recv()
+
+    def halo_tile(q, j):
         p, at = divmod(q, per)
-        if j == 1:
-            inner = mix_send[q] if q < levels else rest_send[q - levels]
-        elif q < levels:
-            inner = mix_recv[j // 2, q]
-        else:
-            inner = rest_recv[q - levels]
         west_part = pltpu.roll(strip_recv[0, j, p], LANES - NEAR - NEAR * at, 1)
         east_part = strip_recv[1, j, p]
         if at:
             east_part = pltpu.roll(east_part, LANES - NEAR * at, 1)
-        return jnp.concatenate([inner, jnp.where(low_half, east_part, west_part)], axis=1)
+        return jnp.where(low_half, east_part, west_part)
+
+    def wide_tile(q, j):
+        return jnp.concatenate([mix_send[q] if j == 1 else mix_recv[q], halo_tile(q, j)], axis=1)
 
     wide = columns + LANES
 
@@ -623,18 +663,22 @@
         speeds = [(means[j, k, 0], means[j, k, 1]) for k in range(levels)]
         upwind = [wide_tile(2 * levels + k, j) > 0.5 for k in range(levels)]
         terms = column_terms(speeds, upwind, tracer_step * wet_all[j * rows : (j + 1) * rows], kappa_in)
-        band = slice(j * rows, (j + 1) * rows)
+        first = lax.broadcasted_iota(jnp.int32, (rows, wide), 0) == 0
+        last = lax.broadcasted_iota(jnp.int32, (rows, wide), 0) == rows - 1
+
+        def row_beside(k, i, side):
+            at = slice(rows - 1, rows) if i == 0 else slice(0, 1)
+            if i == 1:
+                return wide_tile(k, 1)[at]
+            return jnp.concatenate([rows_recv[0, side, pl.ds(cells + k, 1)], halo_tile(k, i)[at]], axis=1)
 
         def heat_cells(k):
-            each = [wide_tile(k, i) for i in range(bands)]
-            d = jnp.concatenate(each, axis=0)
-            return (
-                wide_tile(levels + k, j),
-                pltpu.roll(each[j], 1, 1),
-                pltpu.roll(each[j], wide - 1, 1),
-                pltpu.roll(d, 1, 0)[band],
-                pltpu.roll(d, bands * rows - 1, 0)[band],
-            )
+            d = wide_tile(k, j)
+            south, north = pltpu.roll(d, 1, 0), pltpu.roll(d, rows - 1, 0)
+            if j == 1:
+                south = jnp.where(first, jnp.broadcast_to(row_beside(k, 0, 0), d.shape), south)
+            north = jnp.where(last, jnp.broadcast_to(row_beside(k, j + 1, 1), d.shape), north)
+            return wide_tile(levels + k, j), pltpu.roll(d, 1, 1), pltpu.roll(d, wide - 1, 1), south, north
 
         edges = []
         for k, value in enumerate(solve_column(terms, heat_cells)):
@@ -646,20 +690,9 @@
     heat_band(1)
     hand_on(forces)
 
-    half_wet = tracer_step * wet_cols
-    upwind = [flags[k] == 1 for k in range(levels)]
-    speeds = [tuple(means[1, k, i, :, 0:columns] for i in range(2)) for k in range(levels)]
-    terms = column_terms(speeds, upwind, half_wet, kappa_in)
-    for copy in halo0:
-        copy.wait_recv()
-    shift_cells(0)
-    for i in range(tracers):
-        for k, value in enumerate(solve_column(terms, tracer_cells(i))):
-            conc[i, k] = value
-    halo1 = react_and_pack(1, False)
-    for copy in halo1:
-        copy.start()
-    sent.extend(halo1)
+    @pl.when(me_t != 0)
+    def _():
+        first_tracers()
 
     @pl.when(me_t == 0)
     def _():
@@ -780,7 +813,7 @@
     assert tiles > 3 and sects > 1 and levels == sects * depth and wide == sects * columns
     cells = tracers * levels
     packs = pl.cdiv(cells, LANES)
-    padded = pl.cdiv(cells, 8) * 8
+    padded = pl.cdiv(cells + levels, 8) * 8
     strips = pl.cdiv(3 * levels, LANES // NEAR)
     pair = LANES // (2 * NEAR)
     f32 = jnp.float32
@@ -817,10 +850,8 @@
             pltpu.VMEM((4, sects, 4 * depth, rows, columns), f32),
             pltpu.VMEM((rows, columns), f32),
             pltpu.VMEM((4, rows, columns), f32),
-            pltpu.VMEM((levels, rows, columns), f32),
-            pltpu.VMEM((2, levels, rows, columns), f32),
-            pltpu.VMEM((2 * levels, rows, columns), f32),
-            pltpu.VMEM((2 * levels, rows, columns), f32),
+            pltpu.VMEM((3 * levels, rows, columns), f32),
+            pltpu.VMEM((3 * levels, rows, columns), f32),
             pltpu.VMEM((2, strips, rows, columns), f32),
             pltpu.VMEM((2, 3, strips, rows, columns), f32),
             pltpu.VMEM((3 * rows, columns + LANES), f32),
@@ -836,8 +867,8 @@
             dma((4, sects)),
             dma((4,)),
             dma((4,)),
-            dma((3,)),
-            dma((3,)),
+            dma((1,)),
+            dma((1,)),
             dma((2,)),
             dma((2,)),
             dma((2,)),

time: 20.1 us -> 19.4 us (0.965)
  Pallas kernels: 19.2 us -> 18.3 us
    pallas_call x1, Pallas kernels: 18.5 us -> 17.6 us  [body(): pl.pallas_call(functools.partial(kernel, sects, tiles), out_shape=[pltpu....]
where the time goes in v1:
time: 19.4 us; the launch traced here: 19 us
  Pallas kernels  18.3 us (94%)
  between operations  0.64 us (3%)
    pallas_call x1, Pallas kernels, body(): pl.pallas_call(functools.partial(kernel, sects, tiles), out_shape=[pltpu....  17.6 us
    pallas_call x1, Pallas kernels, body(): pl.pallas_call(put_out, out_shape=[jax.ShapeDtypeStruct(r.shape, f32) for...  0.72 us

profile of v1, /device:TPU:0, one launch (start us, length us, event | category | flops | bytes accessed | tf_op | source)
XLA Modules:
  0.0 19.0 jit_solution(11028354493955943000)
XLA Ops:
  0.6 17.6 %coupled.1 = (f32[12,4,8,128]{3,2,1,0:T(8,128)S(1)}, f32[1,8,512]{2,1,0:T(8,128)S(1)}, f32[1,8,512]{2,1,0:T(8,128)S(1)}, f32[1,8,512]{2,1,0:T(8,128)S(1)}) custom-call(f32[1,8,512]{2,1,0:T(8,128)} %zonal_in.1, f32[1,8,512]{2,1,0:T(8,128)} %merid_in.1, f32[1,8,512]{2,1,0:T(8,128)} %height_in.1, s32[8,512]{1,0:T(8,128)} %sea_in.1, s32[4,8,128]{2,1,0:T(8,128)} %flags_in.1, ...), custom_call_target="tpu_custom_call" | custom-call | tf_op jit(solution)/shard_map/coupled/pallas_call | solution.py:823
  18.3 0.7 %put_out.1 = (f32[12,4,8,128]{3,2,1,0:T(8,128)}, f32[1,8,512]{2,1,0:T(8,128)}, f32[1,8,512]{2,1,0:T(8,128)}, f32[1,8,512]{2,1,0:T(8,128)}) custom-call(f32[12,4,8,128]{3,2,1,0:T(8,128)S(1)} %get-tuple-element.8.refs_0_, f32[1,8,512]{2,1,0:T(8,128)S(1)} %get-tuple-element.9.refs_1_, f32[1,8,512]{2,1,0:T(8,128)S(1)} %get-tuple-element.10.refs_2_, ...), custom_call_target="tpu_custom_call" | custom-call | tf_op jit(solution)/shard_map/put_out/pallas_call | solution.py:887

commit v2 on v1

--- a/solution.py
+++ b/solution.py
@@ -216,15 +216,23 @@
 
     near = sorted(range(sects), key=lambda m: (m.bit_count(), m))
     peers = [(m, across(m), dt, tile_at(dt)) for dt in (1, 0, -1) for m in near if m or dt]
-    mine = place(me_s, me_t)
+    bits = [lax.rem(me_s // (1 << bit), 2) for bit in range((sects - 1).bit_length())]
+    rows_of = {dt: (2 * (t // 2) + 1 - lax.rem(t, 2), t) for dt, t in ((dt, tile_at(dt)) for dt in (1, 0, -1))}
+    hops_of = {m: sum((1 - b if m >> i & 1 else b) for i, b in enumerate(bits)) for m in near}
+    spots = {
+        (m, dt): ((2 * hops_of[m] + rows_of[dt][0]) * tiles + rows_of[dt][1]) * sects + across(m)
+        for m in near
+        for dt in (1, 0, -1)
+    }
+    mine = spots[0, 0]
     later, sooner, direct, answer = [], [], [], []
     for m, s, dt, t in peers:
-        spot = place(s, t)
+        spot = spots[m, dt]
         later.append(spot > mine)
         sooner.append(spot < mine)
         if m and dt:
-            direct.append(spot > place(me_s, t))
-            answer.append((spot < mine) & (mine > place(s, me_t)))
+            direct.append(spot > spots[0, dt])
+            answer.append((spot < mine) & (mine > spots[m, 0]))
         else:
             direct.append(True)
             answer.append(spot < mine)
@@ -576,8 +584,6 @@
         return carry
 
     def beyond_interval(group, carry):
-        for at in range(FIRST):
-            blk_wait(far, group * FIRST + at)
         first_levels(group, (far, 0, 1), jnp.concatenate([wet_band(far), wet_all[0 : 2 * rows]], axis=0), 0)
         return carry
 
@@ -614,7 +620,9 @@
     forces = neighbours(force, force_ssem, force_rsem)
 
     def hand_on(copies):
-        copies[1].start()
+        @pl.when(me_t != 0)
+        def _():
+            copies[1].start()
 
         @pl.when(me_t != tiles - 1)
         def _():
@@ -690,6 +698,11 @@
     heat_band(1)
     hand_on(forces)
 
+    @pl.when(me_t == 0)
+    def _():
+        states[1].start()
+        forces[1].start()
+
     @pl.when(me_t != 0)
     def _():
         first_tracers()
@@ -697,6 +710,8 @@
     @pl.when(me_t == 0)
     def _():
         over[sects].wait_recv()
+        for s in range(sects):
+            blk_wait(far, s)
         lax.fori_loop(0, sects // FIRST, beyond_interval, 0)
         pack_edges(state, 0, [state_edge[0, q] for q in range(3 * levels)])
         rest.wait_recv()
@@ -810,7 +825,7 @@
     tracers, levels, rows, columns = conc.shape
     depth, _, wide = zonal.shape
     assert rows >= NEAR and columns == LANES and INTERVALS == 2
-    assert tiles > 3 and sects > 1 and levels == sects * depth and wide == sects * columns
+    assert tiles > 3 and sects % FIRST == 0 and levels % SECOND == 0 and levels == sects * depth and wide == sects * columns
     cells = tracers * levels
     packs = pl.cdiv(cells, LANES)
     padded = pl.cdiv(cells + levels, 8) * 8

time: 19.4 us -> 19.3 us (level)
  no operation moved by 1% of the time
where the time goes in v2:
time: 19.3 us; the launch traced here: 19 us
  Pallas kernels  18.3 us (95%)
  between operations  0.64 us (3%)
    pallas_call x1, Pallas kernels, body(): pl.pallas_call(functools.partial(kernel, sects, tiles), out_shape=[pltpu....  17.6 us
    pallas_call x1, Pallas kernels, body(): pl.pallas_call(put_out, out_shape=[jax.ShapeDtypeStruct(r.shape, f32) for...  0.72 us

profile of v2, /device:TPU:0, one launch (start us, length us, event | category | flops | bytes accessed | tf_op | source)
XLA Modules:
  0.0 19.0 jit_solution(10991007954357636950)
XLA Ops:
  0.6 17.6 %coupled.1 = (f32[12,4,8,128]{3,2,1,0:T(8,128)S(1)}, f32[1,8,512]{2,1,0:T(8,128)S(1)}, f32[1,8,512]{2,1,0:T(8,128)S(1)}, f32[1,8,512]{2,1,0:T(8,128)S(1)}) custom-call(f32[1,8,512]{2,1,0:T(8,128)} %zonal_in.1, f32[1,8,512]{2,1,0:T(8,128)} %merid_in.1, f32[1,8,512]{2,1,0:T(8,128)} %height_in.1, s32[8,512]{1,0:T(8,128)} %sea_in.1, s32[4,8,128]{2,1,0:T(8,128)} %flags_in.1, ...), custom_call_target="tpu_custom_call" | custom-call | tf_op jit(solution)/shard_map/coupled/pallas_call | solution.py:838
  18.2 0.7 %put_out.1 = (f32[12,4,8,128]{3,2,1,0:T(8,128)}, f32[1,8,512]{2,1,0:T(8,128)}, f32[1,8,512]{2,1,0:T(8,128)}, f32[1,8,512]{2,1,0:T(8,128)}) custom-call(f32[12,4,8,128]{3,2,1,0:T(8,128)S(1)} %get-tuple-element.8.refs_0_, f32[1,8,512]{2,1,0:T(8,128)S(1)} %get-tuple-element.9.refs_1_, f32[1,8,512]{2,1,0:T(8,128)S(1)} %get-tuple-element.10.refs_2_, ...), custom_call_target="tpu_custom_call" | custom-call | tf_op jit(solution)/shard_map/put_out/pallas_call | solution.py:902

commit v3 on v2

--- a/solution.py
+++ b/solution.py
@@ -22,7 +22,7 @@
 EDGE = 4 * STEPS
 NEAR = EDGE // 2
 FIRST = 4
-SECOND = 2
+SECOND = 3
 
 
 def ocean_steps(zonal, merid, height, wet, forced, keep):
@@ -732,7 +732,7 @@
         )
 
     def second_interval(group):
-        for l in [group * SECOND + at for at in range(SECOND)]:
+        for l in group:
             whole = [
                 jnp.concatenate([with_edges(state, j, 3 * l + f, 3 * levels) for j in range(bands)], axis=0)
                 for f in range(3)
@@ -743,14 +743,15 @@
             last_means[l, 1] = mm
             for f, value in enumerate((z, m, h)):
                 out_send[l, f] = value
-        for l in [group * SECOND + at for at in range(SECOND)]:
+        for l in group:
 
             @pl.when(l // depth != me_s)
             def _():
                 out_copy(l).start()
 
-    for group in range(levels // SECOND):
-        second_interval(group)
+    second_interval([0])
+    for start in range(1, levels, SECOND):
+        second_interval(range(start, min(start + SECOND, levels)))
     for ld in range(depth):
         out_recv[me_s, ld] = out_send[me_s * depth + ld]
 
@@ -825,7 +826,7 @@
     tracers, levels, rows, columns = conc.shape
     depth, _, wide = zonal.shape
     assert rows >= NEAR and columns == LANES and INTERVALS == 2
-    assert tiles > 3 and sects % FIRST == 0 and levels % SECOND == 0 and levels == sects * depth and wide == sects * columns
+    assert tiles > 3 and sects % FIRST == 0 and levels == sects * depth and wide == sects * columns
     cells = tracers * levels
     packs = pl.cdiv(cells, LANES)
     padded = pl.cdiv(cells + levels, 8) * 8

time: 19.3 us -> 19.2 us (level)
  no operation moved by 1% of the time
where the time goes in v3:
time: 19.2 us; the launch traced here: 18.9 us
  Pallas kernels  18.3 us (95%)
  between operations  0.64 us (3%)
    pallas_call x1, Pallas kernels, body(): pl.pallas_call(functools.partial(kernel, sects, tiles), out_shape=[pltpu....  17.6 us
    pallas_call x1, Pallas kernels, body(): pl.pallas_call(put_out, out_shape=[jax.ShapeDtypeStruct(r.shape, f32) for...  0.72 us

profile of v3, /device:TPU:0, one launch (start us, length us, event | category | flops | bytes accessed | tf_op | source)
XLA Modules:
  0.0 18.9 jit_solution(9305107734462821726)
XLA Ops:
  0.6 17.6 %coupled.1 = (f32[12,4,8,128]{3,2,1,0:T(8,128)S(1)}, f32[1,8,512]{2,1,0:T(8,128)S(1)}, f32[1,8,512]{2,1,0:T(8,128)S(1)}, f32[1,8,512]{2,1,0:T(8,128)S(1)}) custom-call(f32[1,8,512]{2,1,0:T(8,128)} %zonal_in.1, f32[1,8,512]{2,1,0:T(8,128)} %merid_in.1, f32[1,8,512]{2,1,0:T(8,128)} %height_in.1, s32[8,512]{1,0:T(8,128)} %sea_in.1, s32[4,8,128]{2,1,0:T(8,128)} %flags_in.1, ...), custom_call_target="tpu_custom_call" | custom-call | tf_op jit(solution)/shard_map/coupled/pallas_call | solution.py:839
  18.2 0.7 %put_out.1 = (f32[12,4,8,128]{3,2,1,0:T(8,128)}, f32[1,8,512]{2,1,0:T(8,128)}, f32[1,8,512]{2,1,0:T(8,128)}, f32[1,8,512]{2,1,0:T(8,128)}) custom-call(f32[12,4,8,128]{3,2,1,0:T(8,128)S(1)} %get-tuple-element.8.refs_0_, f32[1,8,512]{2,1,0:T(8,128)S(1)} %get-tuple-element.9.refs_1_, f32[1,8,512]{2,1,0:T(8,128)S(1)} %get-tuple-element.10.refs_2_, ...), custom_call_target="tpu_custom_call" | custom-call | tf_op jit(solution)/shard_map/put_out/pallas_call | solution.py:903
